TPU v7x, 512 devices: a whole 4x8x8 slice. The times are simulated.
512 devices in a mesh: group: 8 (over z), dom: 64 (over y, x, core).
Axes of the slice: x: 4, y: 8, z: 8, core: 2. Of those that a mesh axis runs over, the one named last changes fastest.
Arguments:
- orbitals: bfloat16 [1572864, 512], P(('group', 'dom')), may hold values from -6 to 6
- density_rows: bfloat16 [16384, 2048], P(('group', 'dom')), may hold values from -0.01171875 to 0.01171875
- near_blocks: int32 [512, 32], P(('group', 'dom')), may hold values from 0 to 127, as said below
- leaf_coords: int32 [3, 3072], P(None, ('group', 'dom')), may hold values from 0 to 127, as said below
- near_leaves: int32 [3072, 3], P(('group', 'dom')), may hold values from 0 to 17, as said below
- leaf_basis: float32 [64, 1572864], P(None, ('group', 'dom')), may hold values from -2 to 2
- leaf_transfer: float32 [3072, 64, 64], P(('group', 'dom')), may hold values from -0.75 to 0.75
- dev_transfer: float32 [512, 64, 64], P(('group', 'dom')), may hold values from -0.375 to 0.375
- dev_far: int32 [512, 64], P(('group', 'dom')), may hold values 0 or 1
- group_far: int32 [8, 8], P('group'), may hold values 0 or 1
Outputs:
- density: float32 [1572864], P(('group', 'dom'))
- hartree: float32 [1572864], P(('group', 'dom'))
Inputs may be any that keep to these rules, and one draw needn't show every extreme that they name: `near_blocks`: each row names 32 distinct blocks of its own coarse domain; block b is rows b * 16 to b * 16 + 15 of the domain's density matrix, held by the device of dom index b // 2. The first 2 entries of every row of a domain are the same: all blocks of one device of that domain, in order. Every other entry is a block held by a device whose dom index differs from the row's own by at most 8, counted cyclically over the 64 dom indices. `near_leaves`: each row names 3 distinct window positions, among them the leaf's own position 6 + (t mod 6) for row t. `leaf_coords`: distinct positions for all leaves.
All inputs are finite; a program needn't handle non-finite values. No bound on the sum of `dev_far` or of `group_far` on one device may be relied on, other than what follows from the above.
Results may differ from a plain program's by a relative error of at most 0.0003.
Values may be sent and summed in bfloat16 or wider, within the bound.
A program may use at most 128 MiB of HBM per device.

v0:
```python
import math
import jax
import jax.numpy as jnp
from jax import lax
from jax.sharding import PartitionSpec as P

SIDE = 8
LEAF = 512
CHEB = 4
BW = 16
NEARL = 3
vol_weight = 0.1
soft_square = 1.0


def with_halo(value, sides, width):
    for axis, dim in sides:
        peers, length = (lax.axis_size(axis), value.shape[dim])
        up = [(i, (i + 1) % peers) for i in range(peers - 1)]
        down = [(j, i) for i, j in up]
        last = lax.slice_in_dim(value, length - width, length, axis=dim)
        first = lax.slice_in_dim(value, 0, width, axis=dim)
        before = lax.ppermute(last, axis, up)
        after = lax.ppermute(first, axis, down)
        value = jnp.concatenate([before, value, after], axis=dim)
    return value


def coulomb(target, source):
    diff_x = target[0][:, None] - source[0][None, :]
    diff_y = target[1][:, None] - source[1][None, :]
    diff_z = target[2][:, None] - source[2][None, :]
    return 1.0 / jnp.sqrt(diff_x * diff_x + diff_y * diff_y + diff_z * diff_z + soft_square)


def cluster_nodes(bounds):
    steps_idx = jnp.arange(CHEB).astype(jnp.float32)
    cheb_points = jnp.cos((2.0 * steps_idx + 1.0) * (math.pi / (2.0 * CHEB)))
    centre = 0.5 * (bounds[:3] + bounds[3:])
    half_size = 0.5 * (bounds[3:] - bounds[:3])
    along = centre[:, None] + half_size[:, None] * cheb_points[None, :]
    node_index = jnp.arange(CHEB * CHEB * CHEB)
    first = node_index // (CHEB * CHEB)
    second = node_index // CHEB % CHEB
    third = node_index % CHEB
    return jnp.stack([along[0][first], along[1][second], along[2][third]])


def point_offsets():
    place = jnp.arange(LEAF)
    return jnp.stack([place // (SIDE * SIDE), place // SIDE % SIDE, place % SIDE]).astype(
        jnp.float32
    )


def far_coupling(own_nodes, other_bounds, mask_row, moments):
    other_nodes = jax.vmap(cluster_nodes)(other_bounds)
    coupling = jax.vmap(lambda other: coulomb(own_nodes, other))(other_nodes)
    coupling = coupling * mask_row.astype(jnp.float32)[:, None, None]
    return vol_weight * jnp.einsum("srq,sq->r", coupling, moments, precision=lax.Precision.HIGHEST)


def local(
    orbitals,
    density_rows,
    near_blocks,
    leaf_coords,
    near_leaves,
    leaf_basis,
    leaf_transfer,
    dev_transfer,
    dev_far,
    group_far,
):
    near_list = near_blocks[0]
    near_width = orbitals.shape[1]
    blocks_group = density_rows.shape[1] // BW
    rows_global = (near_list[:, None] * BW + jnp.arange(BW)[None, :]).reshape(-1)
    row_piece = lax.all_gather(density_rows, "dom", axis=0, tiled=True)
    piece_rows = row_piece.shape[0]
    columns = jnp.take(row_piece.reshape(piece_rows, blocks_group, BW), near_list, axis=1).reshape(
        piece_rows, near_width
    )
    inside = (rows_global >= 0) & (rows_global < piece_rows)
    chosen = jnp.take(columns, jnp.clip(rows_global, 0, piece_rows - 1), axis=0)
    local_matrix = jnp.where(
        inside[:, None], chosen, jnp.zeros((near_width, near_width), jnp.bfloat16)
    )
    product = jnp.dot(orbitals, local_matrix, preferred_element_type=jnp.float32)
    density = jnp.sum(product * orbitals.astype(jnp.float32), axis=1)
    leaf_count = leaf_coords.shape[1]
    coords_f = leaf_coords.astype(jnp.float32)
    points = SIDE * coords_f.T[:, :, None] + point_offsets()[None]
    rho_leaf = density.reshape(leaf_count, LEAF)
    packed = jnp.concatenate([points, rho_leaf[:, None, :]], axis=1)
    window = with_halo(packed, (("dom", 0),), leaf_count)

    def near_one(leaf_index):
        own_points = points[leaf_index]
        running = jnp.zeros((LEAF,), jnp.float32)
        for near_slot in range(NEARL):
            source_leaf = window[near_leaves[leaf_index, near_slot]]
            running = running + jnp.dot(
                coulomb(own_points, source_leaf[:3]),
                source_leaf[3],
                precision=lax.Precision.HIGHEST,
            )
        return running

    near_part = lax.map(near_one, jnp.arange(leaf_count)) * vol_weight
    rank = leaf_basis.shape[0]
    leaf_bases = leaf_basis.reshape(rank, leaf_count, LEAF)
    leaf_mom = jnp.einsum("rlp,lp->lr", leaf_bases, rho_leaf, precision=lax.Precision.HIGHEST)
    dev_mom = jnp.einsum("lqr,lq->r", leaf_transfer, leaf_mom, precision=lax.Precision.HIGHEST)
    bounds = jnp.concatenate(
        [SIDE * jnp.min(coords_f, axis=1), SIDE * jnp.max(coords_f, axis=1) + (SIDE - 1)]
    )
    upward = jnp.einsum("qr,q->r", dev_transfer[0], dev_mom, precision=lax.Precision.HIGHEST)
    all_mom, all_bounds = (
        lax.all_gather(dev_mom[None], "dom", axis=0, tiled=True),
        lax.all_gather(bounds[None], "dom", axis=0, tiled=True),
    )
    group_mom = lax.psum(upward, "dom")
    dev_local = far_coupling(cluster_nodes(bounds), all_bounds, dev_far[0], all_mom)
    group_bounds = jnp.concatenate(
        [jnp.min(all_bounds[:, :3], axis=0), jnp.max(all_bounds[:, 3:], axis=0)]
    )
    coarse_mom, coarse_bounds = (
        lax.all_gather(group_mom[None], "group", axis=0, tiled=True),
        lax.all_gather(group_bounds[None], "group", axis=0, tiled=True),
    )
    group_local = far_coupling(cluster_nodes(group_bounds), coarse_bounds, group_far[0], coarse_mom)
    dev_total = dev_local + jnp.einsum(
        "qr,r->q", dev_transfer[0], group_local, precision=lax.Precision.HIGHEST
    )
    leaf_local = jnp.einsum("lqr,r->lq", leaf_transfer, dev_total, precision=lax.Precision.HIGHEST)
    far_part = jnp.einsum("rlp,lr->lp", leaf_bases, leaf_local, precision=lax.Precision.HIGHEST)
    hartree = (near_part + far_part).reshape(-1)
    return (density, hartree)


def solution(mesh):
    in_specs = (
        P(("group", "dom"), None),
        P(("group", "dom"), None),
        P(("group", "dom"), None),
        P(None, ("group", "dom")),
        P(("group", "dom"), None),
        P(None, ("group", "dom")),
        P(("group", "dom"), None, None),
        P(("group", "dom"), None, None),
        P(("group", "dom"), None),
        P("group", None),
    )
    out_specs = (P(("group", "dom")), P(("group", "dom")))
    return jax.shard_map(local, mesh=mesh, in_specs=in_specs, out_specs=out_specs, check_vma=False)
```

profile of v0, /device:TPU:32, one launch (start us, length us, event | category | flops | bytes accessed | tf_op | source)
XLA Modules:
  0.0 532.1 jit_solution(10032816839666519139)
XLA Ops:
  7.2 0.7 all-gather.6.cloned.1.call-update
  7.9 0.7 bitcast_multiply_fusion.1
  8.8 1.3 dynamic-slice.2
  10.1 1.3 dynamic-slice
  13.3 0.7 compare_and_fusion
  14.1 0.8 convert_reduce_fusion.1
  15.3 4.7 copy.52
  20.5 80.6 %all-gather.6.cloned.1.call-done = bf16[2048,2048]{1,0:T(8,128)(2,1)} async-done(((bf16[32,2048]{1,0:T(8,128)(2,1)}), bf16[2048,2048]{1,0:T(8,128)(2,1)}) %all-gather.6.cloned.1.call-update) | async-done | bytes 8388624 | tf_op jit(solution)/shard_map/all_gather | solution.py:79
  101.1 12.3 %copy.50 = bf16[2048,2048]{0,1:T(8,128)(2,1)} copy(bf16[2048,2048]{1,0:T(8,128)(2,1)} %all-gather.6.cloned.1.call-done) | data formatting | bytes 16777216 | tf_op jit(solution)/shard_map/all_gather | solution.py:79
  113.3 4.1 gather_fusion
  117.4 2.5 copy.51
  119.9 1.8 broadcast_select_fusion
  121.7 2.0 gather_fusion.1
  123.7 5.0 fusion.63
  128.8 5.3 %collective-permute-start.1 = (f32[6,4,512]{2,1,0:T(4,128)S(1)}, f32[6,4,512]{2,1,0:T(4,128)S(1)}, u32[]{:S(2)}, u32[]{:S(2)}) collective-permute-start(f32[6,4,512]{2,1,0:T(4,128)S(1)} %pad_maximum_fusion.1), channel_id=1, source_target_pairs={{1,0},{2,1},{3,2},{4,3},{5,4},{6,5},{7,6},{8,7},{9,8},{10,9},{11,1... | collective-permute-start | bytes 147464 | tf_op jit(solution)/shard_map/ppermute | solution.py:24
  134.1 1.9 collective-permute-start
  136.0 0.7 fusion.96
  137.3 251.2 %all-reduce.3 = (f32[4096]{0:T(1024)S(1)}, f32[384]{0:T(512)S(1)}, f32[1,64]{1,0:T(1,128)S(1)}) all-reduce(f32[4096]{0:T(1024)S(1)} %bitcast_dynamic-update-slice_fusion, f32[384]{0:T(512)S(1)} %maximum_dynamic-update-slice_fusion, f32[1,64]{1,0:T(1,128)S(1)} %fusion.126), channel_id=3, replica_groups=mesh['group'=8,'dom'=64] {'dom'}, use_global_device_ids=true, to_apply=%add.1 | all-reduce | flops 4544 | bytes 36352
  388.6 17.1 %all-gather.3 = f32[8,1,64]{2,1,0:T(1,128)S(1)} all-gather(f32[1,1,64]{2,1,0:T(1,128)S(1)} %bitcast.298), channel_id=1, replica_groups=mesh['group'=8,'dom'=64] {'group'}, dimensions={0}, use_global_device_ids=true | all-gather | bytes 2304 | tf_op jit(solution)/shard_map/all_gather | solution.py:129
  406.2 14.9 %all-reduce.2 = f32[48]{0:T(128)S(1)} all-reduce(f32[48]{0:T(128)S(1)} %maximum_dynamic-update-slice_fusion.1), channel_id=4, replica_groups=mesh['group'=8,'dom'=64] {'group'}, use_global_device_ids=true, to_apply=%add.2 | all-reduce | flops 48 | bytes 384
  421.8 0.7 fusion.147
  422.5 0.7 fusion.148
  423.2 0.6 gather_fusion.5
  423.9 0.6 gather_fusion.2
  424.5 0.6 gather_fusion.7
  425.1 0.6 gather_fusion.4
  425.7 0.6 gather_fusion.6
  426.4 0.6 gather_fusion.3
  427.3 2.6 compare_select_fusion.23
  429.9 2.5 compare_select_fusion.24
  432.4 5.0 compare_select_fusion.11
  437.4 5.0 compare_select_fusion.12
  442.9 2.6 fusion.83
  446.8 77.9 %while.10 = (s32[]{:T(128)}, f32[6,512]{1,0:T(8,128)S(1)}, s32[6]{0:T(128)S(1)}, f32[6,3,512]{2,1,0:T(4,128)S(1)}, s32[6,3]{0,1:T(4,128)S(1)}, /*index=5*/f32[18...) while((s32[]{:T(128)}, f32[6,512]{1,0:T(8,128)S(1)}, ...), condition=%wide.region_2.3_spmd, body=%wide.region_1.2_spmd.sunk | while | flops 16516113 | bytes 110989 | solution.py:110
  446.8 0.6 dynamic_slice.31
  449.3 0.6 constant_dynamic-slice_fusion.20
  455.5 1.4 fusion.172
  456.9 1.4 fusion.174
  458.3 1.4 fusion.173
  459.8 0.6 dynamic_slice.31
  462.3 0.6 constant_dynamic-slice_fusion.20
  468.5 1.4 fusion.172
  469.9 1.4 fusion.174
  471.3 1.4 fusion.173
  472.7 0.6 dynamic_slice.31
  475.3 0.6 constant_dynamic-slice_fusion.20
  481.5 1.4 fusion.172
  482.8 1.4 fusion.174
  484.2 1.4 fusion.173
  488.3 0.6 constant_dynamic-slice_fusion.20
  494.4 1.4 fusion.172
  495.8 1.4 fusion.174
  497.2 1.4 fusion.173
  498.7 0.6 dynamic_slice.31
  501.2 0.6 constant_dynamic-slice_fusion.20
  507.4 1.4 fusion.172
  508.8 1.4 fusion.174
  510.2 1.4 fusion.173
  511.7 0.6 dynamic_slice.31
  514.2 0.6 constant_dynamic-slice_fusion.20
  520.4 1.4 fusion.172
  521.8 1.4 fusion.174
  523.2 1.4 fusion.173
  524.7 0.6 reshape.492
  (110 shorter events, 6.4 us)
Async XLA Ops:
  7.2 129.6 %copy-start = (f32[6,64,64]{2,1,0:T(8,128)S(1)}, f32[6,64,64]{2,1,0:T(8,128)}, u32[]{:S(2)}) copy-start(f32[6,64,64]{2,1,0:T(8,128)} %param.18) | copy-start | bytes 294916
  7.2 93.9 %all-gather.6.cloned.1.call-start = ((), (), s32[]{:S(2)}) async-start(), calls=%async_computation | async-start | bytes 8519680 | tf_op jit(solution)/shard_map/all_gather | solution.py:79
  15.2 5.1 copy-start.5
  15.2 5.1 copy-start.6
  15.2 5.1 copy-start.7
  123.7 12.3 %copy-start.1 = (f32[64,3072]{1,0:T(8,128)S(1)}, f32[64,3072]{1,0:T(8,128)}, u32[]{:S(2)}) copy-start(f32[64,3072]{1,0:T(8,128)} %param.17) | copy-start | bytes 2359300
  123.7 13.3 %copy-start.2 = (f32[1,64,64]{2,1,0:T(8,128)S(1)}, f32[1,64,64]{2,1,0:T(8,128)}, u32[]{:S(2)}) copy-start(f32[1,64,64]{2,1,0:T(8,128)} %param.19) | copy-start | bytes 49156
  128.7 318.0 %copy-start.3 = (f32[3072]{0:T(1024)}, f32[3072]{0:T(1024)S(1)}, u32[]{:S(2)}) copy-start(f32[3072]{0:T(1024)S(1)} %fusion.63) | copy-start | bytes 36868
  128.8 317.9 %collective-permute-start.1 = (f32[6,4,512]{2,1,0:T(4,128)S(1)}, f32[6,4,512]{2,1,0:T(4,128)S(1)}, u32[]{:S(2)}, u32[]{:S(2)}) collective-permute-start(f32[6,4,512]{2,1,0:T(4,128)S(1)} %pad_maximum_fusion.1), channel_id=1, source_target_pairs={{1,0},{2,1},{3,2},{4,3},{5,4},{6,5},{7,6},{8,7},{9,8},{10,9},{11,1... | collective-permute-start | bytes 147464 | tf_op jit(solution)/shard_map/ppermute | solution.py:24
  134.1 312.6 %collective-permute-start = (f32[6,4,512]{2,1,0:T(4,128)S(1)}, f32[6,4,512]{2,1,0:T(4,128)S(1)}, u32[]{:S(2)}, u32[]{:S(2)}) collective-permute-start(f32[6,4,512]{2,1,0:T(4,128)S(1)} %pad_maximum_fusion.1), channel_id=1, source_target_pairs={{0,1},{1,2},{2,3},{3,4},{4,5},{5,6},{6,7},{7,8},{8,9},{9,10},{10,1... | collective-permute-start | bytes 147464 | tf_op jit(solution)/shard_map/ppermute | solution.py:23
  442.9 3.9 copy-start.4
Sparse Core Ops, SparseCore 0:
  11.4 89.6 all-gather.5
where the time goes:
time: 534 us; the launch traced here: 532 us
  blocking collectives  283 us (53%)
  waiting for transfers between devices  81.2 us (15%)
  loops' own time  45.1 us (8%)
  local copies, waits for them, and re-layouts  43.1 us (8%)
  matrix products  35.3 us (7%)
  other arithmetic  20.4 us (4%)
  between operations  16.4 us (3%)
  starting transfers between devices  7.29 us (1%)
    unnamed x2, blocking collectives  266 us
    all_gather x1, waiting for transfers between devices, local(): row_piece = lax.all_gather(density_rows, 'dom', axis=0, tiled=True)  80.6 us
    another operation x1, loops' own time, local(): near_part = lax.map(near_one, jnp.arange(leaf_count)) * vol_weight  45.1 us
    dot_general x18, matrix products, near_one(): jnp.dot(coulomb(own_points, source_leaf[:3]), source_leaf[3], precision=l...  25 us
    all_gather x1, blocking collectives, local(): lax.all_gather(group_mom[None], 'group', axis=0, tiled=True)  17.1 us
    gather x7, other arithmetic, cluster_nodes(): return jnp.stack([along[0][first], along[1][second], along[2][third]])  15.1 us
    all_gather x1, local copies, waits for them, and re-layouts, local(): row_piece = lax.all_gather(density_rows, 'dom', axis=0, tiled=True)  12.3 us
  transfers between devices with their start and end apart: 3, of which 1 were waited for; matrix products, arithmetic and copies ran while one was open for 7% of the time, Pallas kernels for 0%

commit v1 on v0

--- a/solution.py
+++ b/solution.py
@@ -3,6 +3,7 @@
 import jax.numpy as jnp
 from jax import lax
 from jax.sharding import PartitionSpec as P
+from jax.lax import all_to_all, axis_size
 
 SIDE = 8
 LEAF = 512
@@ -76,7 +77,16 @@
     near_width = orbitals.shape[1]
     blocks_group = density_rows.shape[1] // BW
     rows_global = (near_list[:, None] * BW + jnp.arange(BW)[None, :]).reshape(-1)
-    row_piece = lax.all_gather(density_rows, "dom", axis=0, tiled=True)
+    _match_streams = lambda point, named_axis: jnp.concatenate(
+        all_to_all(
+            jnp.stack(axis_size(named_axis) * [point]),
+            split_axis=0,
+            axis_name=named_axis,
+            concat_axis=0,
+        ),
+        axis=0,
+    )
+    row_piece = _match_streams(density_rows, "dom")
     piece_rows = row_piece.shape[0]
     columns = jnp.take(row_piece.reshape(piece_rows, blocks_group, BW), near_list, axis=1).reshape(
         piece_rows, near_width

time: 534 us -> 702 us (1.31)
  waiting for transfers between devices: 81.2 us -> 173 us
  local copies, waits for them, and re-layouts: 43.1 us -> 122 us
  between operations: 16.4 us -> 3.03 us
  starting transfers between devices: 7.29 us -> 19.9 us
    all_to_all x0 -> x1, waiting for transfers between devices: none -> 173 us  [local(): all_to_all(jnp.stack(axis_size(named_axis) * [point]), split_axis=0, axis...]
    all_gather x1 -> x0, waiting for transfers between devices: 80.6 us -> none  [local(): row_piece = lax.all_gather(density_rows, 'dom', axis=0, tiled=True)]
    another operation x0 -> x2, local copies, waits for them, and re-layouts: none -> 48.8 us  [the longest x1 43.6 us: local(): row_piece.reshape(piece_rows, blocks_group, BW)]
    all_to_all x0 -> x1, local copies, waits for them, and re-layouts: none -> 44.2 us  [local(): all_to_all(jnp.stack(axis_size(named_axis) * [point]), split_axis=0, axis...]
    all_gather x1 -> x0, local copies, waits for them, and re-layouts: 12.3 us -> none  [local(): row_piece = lax.all_gather(density_rows, 'dom', axis=0, tiled=True)]
    all_to_all x0 -> x1, starting transfers between devices: none -> 11.1 us  [local(): all_to_all(jnp.stack(axis_size(named_axis) * [point]), split_axis=0, axis...]
  transfers between devices with their start and end apart: 3 -> 3, of which waited for: 1 -> 1; matrix products, arithmetic and copies ran while one was open for 7% -> 5% of each run, Pallas kernels for 0% -> 0%
where the time goes in v1:
time: 702 us; the launch traced here: 700 us
  blocking collectives  283 us (40%)
  waiting for transfers between devices  173 us (25%)
  local copies, waits for them, and re-layouts  122 us (17%)
  loops' own time  45 us (6%)
  matrix products  35.3 us (5%)
  starting transfers between devices  19.9 us (3%)
  other arithmetic  18.3 us (3%)
    unnamed x2, blocking collectives  270 us
    all_to_all x1, waiting for transfers between devices, local(): all_to_all(jnp.stack(axis_size(named_axis) * [point]), split_axis=0, axis...  173 us
    another operation x1, loops' own time, local(): near_part = lax.map(near_one, jnp.arange(leaf_count)) * vol_weight  45 us
    all_to_all x1, local copies, waits for them, and re-layouts, local(): all_to_all(jnp.stack(axis_size(named_axis) * [point]), split_axis=0, axis...  44.2 us
    another operation x1, local copies, waits for them, and re-layouts, local(): row_piece.reshape(piece_rows, blocks_group, BW)  43.6 us
    dot_general x18, matrix products, near_one(): jnp.dot(coulomb(own_points, source_leaf[:3]), source_leaf[3], precision=l...  25 us
    gather x7, other arithmetic, cluster_nodes(): return jnp.stack([along[0][first], along[1][second], along[2][third]])  15.1 us
  transfers between devices with their start and end apart: 3, of which 1 were waited for; matrix products, arithmetic and copies ran while one was open for 5% of the time, Pallas kernels for 0%

profile of v1, /device:TPU:32, one launch (start us, length us, event | category | flops | bytes accessed | tf_op | source)
XLA Modules:
  0.0 700.1 jit_solution(8062636788484208269)
XLA Ops:
  0.6 5.2 stack.20
  5.9 11.1 %all-to-all-start = ((bf16[64,32,2048]{2,1,0:T(8,128)(2,1)}), bf16[64,32,2048]{2,1,0:T(8,128)(2,1)}, u32[]{:S(2)}, u32[]{:S(2)}) async-start(bf16[64,32,2048]{2,1,0:T(8,128)(2,1)} %stack.20), calls=%async_computation | async-start | bytes 16777216 | tf_op jit(solution)/shard_map/all_to_all | solution.py:81
  17.6 3.0 copy.52
  20.7 1.3 dynamic-slice
  23.2 1.3 dynamic-slice.2
  26.0 173.2 %all-to-all-done = bf16[64,32,2048]{2,1,0:T(8,128)(2,1)} async-done(((bf16[64,32,2048]{2,1,0:T(8,128)(2,1)}), bf16[64,32,2048]{2,1,0:T(8,128)(2,1)}, u32[]{:S(2)}, u32[]{:S(2)}) %all-to-all-start) | async-done | bytes 8388640 | tf_op jit(solution)/shard_map/all_to_all | solution.py:81
  199.2 44.2 %copy.50 = bf16[64,32,2048]{1,0,2:T(8,128)(2,1)} copy(bf16[64,32,2048]{2,1,0:T(8,128)(2,1)} %all-to-all-done) | data formatting | bytes 16777216 | tf_op jit(solution)/shard_map/all_to_all | solution.py:81
  243.4 43.6 %reshape_reshape.3 = bf16[2048,128,16]{0,2,1:T(8,128)(2,1)} reshape(bf16[64,32,2048]{1,0,2:T(8,128)(2,1)} %copy.50) | data formatting | bytes 16777216 | tf_op jit(solution)/shard_map/reshape;reshape | solution.py:91
  287.0 4.1 gather_fusion
  291.1 2.5 copy.51
  293.6 1.8 broadcast_select_fusion
  295.4 2.0 gather_fusion.1
  297.4 5.0 fusion.63
  302.4 1.9 collective-permute-start
  304.3 7.0 collective-permute-start.1
  311.3 0.7 fusion.96
  312.6 246.2 %all-reduce.3 = (f32[4096]{0:T(1024)S(1)}, f32[384]{0:T(512)S(1)}, f32[1,64]{1,0:T(1,128)S(1)}) all-reduce(f32[4096]{0:T(1024)S(1)} %bitcast_dynamic-update-slice_fusion, f32[384]{0:T(512)S(1)} %maximum_dynamic-update-slice_fusion, f32[1,64]{1,0:T(1,128)S(1)} %fusion.126), channel_id=3, replica_groups=mesh['group'=8,'dom'=64] {'dom'}, use_global_device_ids=true, to_apply=%add.1 | all-reduce | flops 4544 | bytes 36352
  559.1 0.7 fusion.147
  560.0 23.4 %all-reduce.2 = f32[48]{0:T(128)S(1)} all-reduce(f32[48]{0:T(128)S(1)} %maximum_dynamic-update-slice_fusion.1), channel_id=4, replica_groups=mesh['group'=8,'dom'=64] {'group'}, use_global_device_ids=true, to_apply=%add.2 | all-reduce | flops 48 | bytes 384
  583.8 0.6 gather_fusion.5
  584.4 0.6 gather_fusion.6
  585.1 0.6 gather_fusion.7
  585.8 13.4 %all-gather.3 = f32[8,1,64]{2,1,0:T(1,128)S(1)} all-gather(f32[1,1,64]{2,1,0:T(1,128)S(1)} %bitcast.298), channel_id=1, replica_groups=mesh['group'=8,'dom'=64] {'group'}, dimensions={0}, use_global_device_ids=true | all-gather | bytes 2304 | tf_op jit(solution)/shard_map/all_gather | solution.py:139
  599.2 0.7 fusion.148
  600.1 0.6 gather_fusion.2
  600.7 0.6 gather_fusion.3
  601.3 0.6 gather_fusion.4
  602.3 2.5 compare_select_fusion.23
  604.8 2.5 compare_select_fusion.24
  607.2 4.9 compare_select_fusion.11
  612.6 5.2 compare_select_fusion.12
  617.8 2.5 fusion.83
  621.7 77.8 %while.10 = (s32[]{:T(128)}, f32[6,512]{1,0:T(8,128)S(1)}, s32[6]{0:T(128)S(1)}, f32[6,3,512]{2,1,0:T(4,128)S(1)}, s32[6,3]{0,1:T(4,128)S(1)}, /*index=5*/f32[18...) while((s32[]{:T(128)}, f32[6,512]{1,0:T(8,128)S(1)}, ...), condition=%wide.region_2.3_spmd, body=%wide.region_1.2_spmd.sunk | while | flops 16516113 | bytes 110981 | solution.py:120
  621.7 0.6 dynamic_slice.31
  624.2 0.6 constant_dynamic-slice_fusion.20
  630.4 1.4 fusion.174
  631.8 1.4 fusion.173
  633.2 1.4 fusion.172
  634.7 0.6 dynamic_slice.31
  637.2 0.6 constant_dynamic-slice_fusion.20
  643.4 1.4 fusion.174
  644.8 1.4 fusion.173
  646.2 1.4 fusion.172
  647.6 0.6 dynamic_slice.31
  650.2 0.6 constant_dynamic-slice_fusion.20
  656.4 1.4 fusion.174
  657.7 1.4 fusion.173
  659.1 1.4 fusion.172
  660.6 0.6 dynamic_slice.31
  663.1 0.6 constant_dynamic-slice_fusion.20
  669.3 1.4 fusion.174
  670.7 1.4 fusion.173
  672.1 1.4 fusion.172
  673.6 0.6 dynamic_slice.31
  676.1 0.6 constant_dynamic-slice_fusion.20
  682.3 1.4 fusion.174
  683.7 1.4 fusion.173
  685.1 1.4 fusion.172
  686.6 0.6 dynamic_slice.31
  689.1 0.6 constant_dynamic-slice_fusion.20
  695.3 1.4 fusion.174
  696.7 1.4 fusion.173
  698.0 1.4 fusion.172
  699.5 0.6 reshape.490
  (115 shorter events, 5.8 us)
Async XLA Ops:
  0.6 311.4 %copy-start = (f32[6,64,64]{2,1,0:T(8,128)S(1)}, f32[6,64,64]{2,1,0:T(8,128)}, u32[]{:S(2)}) copy-start(f32[6,64,64]{2,1,0:T(8,128)} %param.18) | copy-start | bytes 294916
  5.9 11.1 %copy-start.7 = (s32[1,32]{1,0:T(1,128)S(1)}, s32[1,32]{1,0:T(1,128)}, u32[]{:S(2)}) copy-start(s32[1,32]{1,0:T(1,128)} %param.14) | copy-start | bytes 388
  5.9 11.7 %copy-start.1 = (bf16[3072,512]{1,0:T(8,128)(2,1)S(1)}, bf16[3072,512]{1,0:T(8,128)(2,1)}, u32[]{:S(2)}) copy-start(bf16[3072,512]{1,0:T(8,128)(2,1)} %param.12) | copy-start | bytes 9437188
  5.9 193.3 %all-to-all-start = ((bf16[64,32,2048]{2,1,0:T(8,128)(2,1)}), bf16[64,32,2048]{2,1,0:T(8,128)(2,1)}, u32[]{:S(2)}, u32[]{:S(2)}) async-start(bf16[64,32,2048]{2,1,0:T(8,128)(2,1)} %stack.20), calls=%async_computation | async-start | bytes 16777216 | tf_op jit(solution)/shard_map/all_to_all | solution.py:81
  17.6 7.6 %copy-start.6 = (s32[3,6]{1,0:T(4,128)S(1)}, s32[3,6]{1,0:T(4,128)}, u32[]{:S(2)}) copy-start(s32[3,6]{1,0:T(4,128)} %param.15) | copy-start | bytes 220
  17.6 8.2 %copy-start.8 = (s32[1,8]{1,0:T(1,128)S(1)}, s32[1,8]{1,0:T(1,128)}, u32[]{:S(2)}) copy-start(s32[1,8]{1,0:T(1,128)} %param.21) | copy-start | bytes 100
  17.6 8.3 %copy-start.9 = (s32[1,64]{1,0:T(1,128)S(1)}, s32[1,64]{1,0:T(1,128)}, u32[]{:S(2)}) copy-start(s32[1,64]{1,0:T(1,128)} %param.20) | copy-start | bytes 772
  297.4 14.0 %copy-start.2 = (f32[64,3072]{1,0:T(8,128)S(1)}, f32[64,3072]{1,0:T(8,128)}, u32[]{:S(2)}) copy-start(f32[64,3072]{1,0:T(8,128)} %param.17) | copy-start | bytes 2359300
  297.4 15.0 %copy-start.3 = (f32[1,64,64]{2,1,0:T(8,128)S(1)}, f32[1,64,64]{2,1,0:T(8,128)}, u32[]{:S(2)}) copy-start(f32[1,64,64]{2,1,0:T(8,128)} %param.19) | copy-start | bytes 49156
  302.4 319.2 %copy-start.4 = (f32[3072]{0:T(1024)}, f32[3072]{0:T(1024)S(1)}, u32[]{:S(2)}) copy-start(f32[3072]{0:T(1024)S(1)} %fusion.63) | copy-start | bytes 36868
  302.4 319.2 %collective-permute-start = (f32[6,4,512]{2,1,0:T(4,128)S(1)}, f32[6,4,512]{2,1,0:T(4,128)S(1)}, u32[]{:S(2)}, u32[]{:S(2)}) collective-permute-start(f32[6,4,512]{2,1,0:T(4,128)S(1)} %pad_maximum_fusion.1), channel_id=1, source_target_pairs={{0,1},{1,2},{2,3},{3,4},{4,5},{5,6},{6,7},{7,8},{8,9},{9,10},{10,1... | collective-permute-start | bytes 147464 | tf_op jit(solution)/shard_map/ppermute | solution.py:24
  304.3 317.2 %collective-permute-start.1 = (f32[6,4,512]{2,1,0:T(4,128)S(1)}, f32[6,4,512]{2,1,0:T(4,128)S(1)}, u32[]{:S(2)}, u32[]{:S(2)}) collective-permute-start(f32[6,4,512]{2,1,0:T(4,128)S(1)} %pad_maximum_fusion.1), channel_id=1, source_target_pairs={{1,0},{2,1},{3,2},{4,3},{5,4},{6,5},{7,6},{8,7},{9,8},{10,9},{11,1... | collective-permute-start | bytes 147464 | tf_op jit(solution)/shard_map/ppermute | solution.py:25
  617.8 3.9 copy-start.5
